TPU v7x, 256 devices: a whole 4x4x8 slice. The times are simulated.
256 devices in a mesh: sens: 8 (over z_lo, core), pts: 32 (over y, z_hi, x).
Axes of the slice: x: 4, y: 4, z: 8 (z_hi: 2, z_lo: 4; z = z_hi * 4 + z_lo), core: 2. Of those that a mesh axis runs over, the one named last changes fastest.
Arguments:
- kernel: float32 [64, 2048, 384], P('sens', 'pts'), may hold values from -0.0068359375 to 0.0068359375
- vectors: float32 [8, 2048, 384], P(None, 'pts'), may hold values from -6 to 6
- noise_scale: float32 [64], P('sens'), may hold values from 0.5 to 2
- sensor_group: int32 [64], P('sens'), may hold values from 0 to 3
- correlation: float32 [4, 384, 384], replicated, may hold values from -0.3125 to 0.3125
- stiffness: float32 [2048], P('pts'), may hold values from 0.2 to 1
- couplings: float32 [4, 2048], P(None, 'pts'), may hold values from 0.05 to 0.5
- neighbors: int32 [4, 2048], P(None, 'pts'), may hold values from 0 to 2047, as said below
Outputs:
- hessian_action: float32 [8, 2048, 384], P('sens', 'pts')
Inputs may be any that keep to these rules, and one draw needn't show every extreme that they name: `neighbors`: points are numbered row by row on a grid of rows of 16 points; every neighbor of point p lies in p's grid row or in one of the two rows beside it.
All inputs are finite; a program needn't handle non-finite values.
Results may differ from a plain program's by a relative error of at most 0.0001.
Values sent between devices are 32-bit elements; how exact they have to be, the bound alone decides.
A program may use at most 64 MiB of HBM per device.

v0:
```python
import math
import jax
import jax.numpy as jnp
from jax import lax
from jax.sharding import PartitionSpec as P

COLS = 16
HIGHEST = lax.Precision.HIGHEST


def padded_2(block, sides, width):
    for axis, dim in sides:
        count = lax.axis_size(axis)
        forward = [(i, i + 1) for i in range(count - 1)]
        backward = [(target, source) for source, target in forward]
        low = lax.ppermute(
            lax.slice_in_dim(block, block.shape[dim] - width, None, axis=dim), axis, forward
        )
        high = lax.ppermute(lax.slice_in_dim(block, 0, width, axis=dim), axis, backward)
        block = jnp.concatenate([low, block, high], axis=dim)
    return block


def tables(length):
    span = 2 * length
    steps = lax.iota(jnp.int32, length)
    phase = steps[:, None] * steps[None, :] % span
    angle = phase.astype(jnp.float32) * (2.0 * math.pi / span)
    cosine = jnp.cos(angle)
    sine = jnp.sin(angle)
    nyquist = jnp.where(steps % 2 == 0, 1.0, -1.0).astype(jnp.float32)
    first_col = steps == 0
    second = jnp.where(first_col[None, :], nyquist[:, None], -sine)
    forward = jnp.concatenate([cosine, second], axis=1)
    weight = jnp.where(first_col, 1.0, 2.0).astype(jnp.float32)
    back_first = cosine * weight[:, None]
    back_second = jnp.where(first_col[:, None], nyquist[None, :], -2.0 * sine)
    inverse = jnp.concatenate([back_first, back_second], axis=0) / span
    return (forward, inverse)


def spectral(left, right, form, half):
    left_x, left_y = (left[..., :half], left[..., half:])
    right_x, right_y = (right[..., :half], right[..., half:])
    prod_xx = jnp.einsum(form, left_x, right_x, precision=HIGHEST)
    prod_yy = jnp.einsum(form, left_y, right_y, precision=HIGHEST)
    prod_xy = jnp.einsum(form, left_x, right_y, precision=HIGHEST)
    prod_yx = jnp.einsum(form, left_y, right_x, precision=HIGHEST)
    keep = (lax.iota(jnp.int32, half) > 0).astype(jnp.float32)
    real_part = prod_xx - keep * prod_yy
    imag_part = keep * (prod_xy + prod_yx) + (1.0 - keep) * prod_yy
    return jnp.concatenate([real_part, imag_part], axis=-1)


def weight_rows(rows, row_ids, noise_scale, sensor_group, correlation):
    sensors = noise_scale.shape[0]
    groups = correlation.shape[0]
    pick = (row_ids[:, None] % sensors == lax.iota(jnp.int32, sensors)[None, :]).astype(jnp.float32)
    group_table = (sensor_group[:, None] == lax.iota(jnp.int32, groups)[None, :]).astype(
        jnp.float32
    )
    row_scale = jnp.dot(pick, noise_scale, precision=HIGHEST)
    row_group = jnp.dot(pick, group_table, precision=HIGHEST)
    mixed = jnp.einsum("rt,but->rbu", rows, correlation, precision=HIGHEST)
    extra = jnp.einsum("rbu,rb->ru", mixed, row_group, precision=HIGHEST)
    return row_scale[:, None] * (rows + extra)


def local(kernel, vectors, noise_scale, sensor_group, correlation, stiffness, couplings, neighbors):
    sensors, points, length = kernel.shape
    count = vectors.shape[0]
    forward, inverse = tables(length)
    kern_hat = jnp.einsum("spt,tf->spf", kernel, forward, precision=HIGHEST)
    vec_hat = jnp.einsum("kpt,tf->kpf", vectors, forward, precision=HIGHEST)
    pred_hat = spectral(vec_hat, kern_hat, "kpf,spf->ksf", length)
    partial_value = jnp.einsum("ksf,ft->kst", pred_hat, inverse, precision=HIGHEST)
    flat = partial_value.reshape(count * sensors, length)
    predicted = lax.psum(flat, "pts")
    row_ids = lax.iota(jnp.int32, count * sensors)
    weighted = weight_rows(predicted, row_ids, noise_scale, sensor_group, correlation)
    residual = weighted.reshape(count, sensors, length)
    res_hat = jnp.einsum("kst,tf->ksf", residual, forward, precision=HIGHEST)
    columns = lax.iota(jnp.int32, 2 * length)
    flip = jnp.where(columns > length, -1.0, 1.0).astype(jnp.float32)
    conj_hat = kern_hat * flip
    grad_hat = spectral(res_hat, conj_hat, "ksf,spf->kpf", length)
    own_count = count // lax.axis_size("sens")
    data_term = lax.psum_scatter(
        jnp.einsum("kpf,ft->kpt", grad_hat, inverse, precision=HIGHEST),
        "sens",
        scatter_dimension=0,
        tiled=True,
    )
    own_vectors = lax.dynamic_slice_in_dim(
        vectors, lax.axis_index("sens") * own_count, own_count, 0
    )
    padded = padded_2(own_vectors, (("pts", 1),), COLS)
    local_index = neighbors - lax.axis_index("pts") * points + COLS
    gathered = jnp.take(padded, local_index, axis=1)
    prior_term = stiffness[None, :, None] * own_vectors
    prior_term = prior_term + jnp.sum(
        couplings[None, :, :, None] * (own_vectors[:, None] - gathered), axis=1
    )
    return data_term + prior_term


def solution(mesh):
    in_specs = (
        P("sens", "pts", None),
        P(None, "pts", None),
        P("sens"),
        P("sens"),
        P(),
        P("pts"),
        P(None, "pts"),
        P(None, "pts"),
    )
    out_specs = P("sens", "pts", None)
    return jax.shard_map(local, mesh=mesh, in_specs=in_specs, out_specs=out_specs, check_vma=False)
```

profile of v0, /device:TPU:12, one launch (start us, length us, event | category | flops | bytes accessed | tf_op | source)
XLA Modules:
  0.0 537.6 jit_solution(15899717636893823764)
XLA Ops:
  8.8 3.3 multiply_select_fusion
  12.2 2.7 broadcast_multiply_fusion
  16.7 2.8 copy.15
  19.4 3.8 convolution_bitcast_fusion
  24.6 2.8 copy.16
  27.4 2.8 copy.23
  30.2 5.8 %fusion.51 = f32[384,8,8]{2,1,0:T(8,128)} fusion(f32[8,64,384]{1,0,2:T(8,128)} %copy.15, f32[8,64,384]{1,0,2:T(8,128)} %copy.16), kind=kOutput, calls=%fused_computation.86 | convolution fusion | flops 18874368 | bytes 1671168 | tf_op jit(solution)/shard_map/kpf,spf->ksf/dot_general | solution.py:46
  36.1 4.0 fusion.52
  40.1 2.9 copy.22
  43.0 6.4 %subtract_bitcast_fusion.1 = f32[8,8,384]{0,1,2:T(8,128)} fusion(f32[384,8,8]{2,1,0:T(8,128)} %fusion.51, f32[8,64,384]{1,0,2:T(8,128)} %copy.22, f32[8,64,384]{1,0,2:T(8,128)} %copy.23, f32[384]{0:T(512)S(1)} %fusion.38), kind=kOutput, calls=%fused_computation.7 | convolution fusion | flops 18923520 | bytes 1771008 | tf_op jit(solution)/shard_map/kpf,spf->ksf/dot_general | solution.py:45
  49.4 4.4 add_bitcast_fusion.1
  56.2 2.5 copy.17
  61.8 2.6 convolution_bitcast_fusion.2
  65.5 2.8 copy.19
  68.3 2.8 copy.27
  73.4 370.9 %all-reduce.2.cloned.1.call-done = f32[64,384]{1,0:T(8,128)} async-done(((f32[64,384]{1,0:T(8,128)}), f32[64,384]{1,0:T(8,128)}) %all-reduce.2.cloned.1.call-update) | async-done | bytes 98320 | tf_op jit(solution)/shard_map/psum | solution.py:78
  444.3 3.4 fusion.24
  453.2 5.4 fusion.53
  458.5 3.5 fusion.54
  462.1 3.6 subtract_bitcast_fusion
  465.7 4.2 add_bitcast_fusion
  471.1 6.6 %fusion = f32[8,64,384]{2,1,0:T(8,128)} fusion(f32[8,64,768]{1,0,2:T(8,128)S(1)} %pad_maximum_fusion, f32[384,384]{1,0:T(8,128)S(1)} %copy-done.13, f32[384,384]{1,0:T(8,128)S(1)} %copy-done.12), kind=kOutput, calls=%fused_computation.2 | convolution fusion | flops 1812529152 | bytes 3538944 | tf_op jit(solution)/shard_map/kpf,ft->kpt/dot_general | solution.py:89
  480.4 3.9 collective-permute-start.1
  488.2 40.6 %reduce-scatter.2.cloned.1.call-done = f32[1,64,384]{2,1,0:T(8,128)} async-done(((f32[8,64,384]{2,1,0:T(8,128)}), f32[1,64,384]{2,1,0:T(8,128)}) %reduce-scatter.2.cloned.1.call-update) | async-done | bytes 98320 | tf_op jit(solution)/shard_map/reduce_scatter | solution.py:88
  (81 shorter events, 29.1 us)
Async XLA Ops:
  6.5 437.8 %copy-start = (f32[4,384,384]{2,1,0:T(8,128)S(1)}, f32[4,384,384]{2,1,0:T(8,128)}, u32[]{:S(2)}) copy-start(f32[4,384,384]{2,1,0:T(8,128)} %param.12) | copy-start | bytes 7077892
  6.5 437.8 %all-reduce.2.cloned.1.call-start = ((), (), s32[]{:S(2)}) async-start(), calls=%async_computation.1 | async-start | bytes 196608 | tf_op jit(solution)/shard_map/psum | solution.py:78
  6.5 5.6 %copy-start.14 = (f32[8,64,384]{2,1,0:T(8,128)S(1)}, f32[8,64,384]{2,1,0:T(8,128)}, u32[]{:S(2)}) copy-start(f32[8,64,384]{2,1,0:T(8,128)} %param.8) | copy-start | bytes 2359300
  30.2 5.9 %copy-start.7 = (f32[8,64,384]{1,0,2:T(8,128)S(1)}, f32[8,64,384]{1,0,2:T(8,128)}, u32[]{:S(2)}) copy-start(f32[8,64,384]{1,0,2:T(8,128)} %copy.15) | copy-start | bytes 2359300
  30.2 5.9 %copy-start.8 = (f32[8,64,384]{1,0,2:T(8,128)S(1)}, f32[8,64,384]{1,0,2:T(8,128)}, u32[]{:S(2)}) copy-start(f32[8,64,384]{1,0,2:T(8,128)} %copy.23) | copy-start | bytes 2359300
  43.0 6.4 %copy-start.3 = (f32[8,64,384]{1,0,2:T(8,128)S(1)}, f32[8,64,384]{1,0,2:T(8,128)}, u32[]{:S(2)}) copy-start(f32[8,64,384]{1,0,2:T(8,128)} %copy.16) | copy-start | bytes 2359300
  43.0 6.4 %copy-start.4 = (f32[384,8,8]{2,1,0:T(8,128)S(1)}, f32[384,8,8]{2,1,0:T(8,128)}, u32[]{:S(2)}) copy-start(f32[384,8,8]{2,1,0:T(8,128)} %fusion.51) | copy-start | bytes 294916
  43.0 6.4 %copy-start.5 = (f32[8,64,384]{1,0,2:T(8,128)S(1)}, f32[8,64,384]{1,0,2:T(8,128)}, u32[]{:S(2)}) copy-start(f32[8,64,384]{1,0,2:T(8,128)} %copy.22) | copy-start | bytes 2359300
  43.0 6.4 %copy-start.10 = (f32[384,8,8]{2,1,0:T(8,128)S(1)}, f32[384,8,8]{2,1,0:T(8,128)}, u32[]{:S(2)}) copy-start(f32[384,8,8]{2,1,0:T(8,128)} %fusion.52) | copy-start | bytes 294916
  64.4 464.4 %reduce-scatter.2.cloned.1.call-start = ((), (), s32[]{:S(2)}) async-start(), calls=%async_computation.2 | async-start | bytes 884736 | tf_op jit(solution)/shard_map/reduce_scatter | solution.py:88
  68.3 2.8 copy-start.20
  68.3 4.3 copy-start.21
  444.3 3.4 copy-start.16
  444.3 4.6 copy-start.15
  453.1 5.4 copy-start.6
  453.2 5.4 %copy-start.9 = (f32[8,8,384]{0,1,2:T(8,128)S(1)}, f32[8,8,384]{0,1,2:T(8,128)}, u32[]{:S(2)}) copy-start(f32[8,8,384]{0,1,2:T(8,128)} %copy.28) | copy-start | bytes 294916
  458.5 3.5 copy-start.1
  462.1 3.6 copy-start.2
  469.9 1.1 copy-start.12
  469.9 1.2 copy-start.13
  471.1 13.3 %copy-start.18 = (s32[4,64]{1,0:T(4,128)S(1)}, s32[4,64]{1,0:T(4,128)}, u32[]{:S(2)}) copy-start(s32[4,64]{1,0:T(4,128)} %param.15) | copy-start | bytes 3076
  478.5 7.8 %collective-permute-start = (f32[1,16,384]{2,1,0:T(8,128)S(1)}, f32[1,16,384]{2,1,0:T(8,128)S(1)}, u32[]{:S(2)}, u32[]{:S(2)}) collective-permute-start(f32[1,16,384]{2,1,0:T(8,128)S(1)} %get-tuple-element.13), channel_id=1, source_target_pairs={{0,1},{1,2},{2,3},{3,4},{4,5},{5,6},{6,7},{7,8},{8,9},{9,10},{10,1... | collective-permute-start | bytes 73736 | tf_op jit(solution)/shard_map/ppermute | solution.py:16
  480.4 6.6 %collective-permute-start.1 = (f32[1,16,384]{2,1,0:T(8,128)S(1)}, f32[1,16,384]{2,1,0:T(8,128)S(1)}, u32[]{:S(2)}, u32[]{:S(2)}) collective-permute-start(f32[1,16,384]{2,1,0:T(8,128)S(1)} %get-tuple-element.14), channel_id=1, source_target_pairs={{1,0},{2,1},{3,2},{4,3},{5,4},{6,5},{7,6},{8,7},{9,8},{10,9},{11,1... | collective-permute-start | bytes 73736 | tf_op jit(solution)/shard_map/ppermute | solution.py:19
  487.1 41.8 %copy-start.19 = (f32[64]{0:T(128)S(1)}, f32[64]{0:T(128)}, u32[]{:S(2)}) copy-start(f32[64]{0:T(128)} %param.13) | copy-start | bytes 772
  (2 other events, 1.8 us)
Sparse Core Ops, SparseCore 0:
  64.6 379.6 all-reduce.1
  477.9 50.9 reduce-scatter.1
where the time goes:
time: 541 us; the launch traced here: 538 us
  waiting for transfers between devices  412 us (76%)
  matrix products  60.8 us (11%)
  local copies, waits for them, and re-layouts  33.8 us (6%)
  between operations  13.9 us (3%)
  other arithmetic  10.4 us (2%)
  starting transfers between devices  6.28 us (1%)
    psum x1, waiting for transfers between devices, local(): predicted = lax.psum(flat, 'pts')  371 us
    reduce_scatter x1, waiting for transfers between devices, local(): lax.psum_scatter(jnp.einsum('kpf,ft->kpt', grad_hat, inverse, precision=H...  40.6 us
    slice x5, local copies, waits for them, and re-layouts, spectral(): right_x, right_y = (right[..., :half], right[..., half:])  13 us
    dot_general x2, matrix products, spectral(): prod_yy = jnp.einsum(form, left_y, right_y, precision=HIGHEST)  11.2 us
  transfers between devices with their start and end apart: 4, of which 3 were waited for; matrix products, arithmetic and copies ran while one was open for 2% of the time, Pallas kernels for 0%

commit v1 on v0

--- a/solution.py
+++ b/solution.py
@@ -75,7 +75,7 @@
     pred_hat = spectral(vec_hat, kern_hat, "kpf,spf->ksf", length)
     partial_value = jnp.einsum("ksf,ft->kst", pred_hat, inverse, precision=HIGHEST)
     flat = partial_value.reshape(count * sensors, length)
-    predicted = lax.psum(flat, "pts")
+    predicted = jnp.sum(lax.all_gather(flat, "pts"), axis=0)
     row_ids = lax.iota(jnp.int32, count * sensors)
     weighted = weight_rows(predicted, row_ids, noise_scale, sensor_group, correlation)
     residual = weighted.reshape(count, sensors, length)

time: 541 us -> 248 us (0.46)
  waiting for transfers between devices: 412 us -> 118 us
    psum x1 -> x0, waiting for transfers between devices: 371 us -> none  [local(): predicted = lax.psum(flat, 'pts')]
    all_gather x0 -> x1, waiting for transfers between devices: none -> 93.9 us  [local(): predicted = jnp.sum(lax.all_gather(flat, 'pts'), axis=0)]
    reduce_scatter x1, waiting for transfers between devices: 40.6 us -> 22.7 us  [local(): lax.psum_scatter(jnp.einsum('kpf,ft->kpt', grad_hat, inverse, precision=H...]
  transfers between devices with their start and end apart: 4 -> 4, of which waited for: 3 -> 3; matrix products, arithmetic and copies ran while one was open for 2% -> 5% of each run, Pallas kernels for 0% -> 0%
where the time goes in v1:
time: 248 us; the launch traced here: 244 us
  waiting for transfers between devices  118 us (48%)
  matrix products  60.1 us (24%)
  local copies, waits for them, and re-layouts  33.8 us (14%)
  between operations  13.9 us (6%)
  other arithmetic  12.6 us (5%)
  starting transfers between devices  6.28 us (3%)
    all_gather x1, waiting for transfers between devices, local(): predicted = jnp.sum(lax.all_gather(flat, 'pts'), axis=0)  93.9 us
    reduce_scatter x1, waiting for transfers between devices, local(): lax.psum_scatter(jnp.einsum('kpf,ft->kpt', grad_hat, inverse, precision=H...  22.7 us
    slice x5, local copies, waits for them, and re-layouts, spectral(): right_x, right_y = (right[..., :half], right[..., half:])  13 us
    dot_general x2, matrix products, spectral(): prod_yy = jnp.einsum(form, left_y, right_y, precision=HIGHEST)  11.2 us
    slice x6, local copies, waits for them, and re-layouts, spectral(): left_x, left_y = (left[..., :half], left[..., half:])  10.3 us
    dot_general x2, matrix products, spectral(): prod_xx = jnp.einsum(form, left_x, right_x, precision=HIGHEST)  9.99 us
    dot_general x2, matrix products, spectral(): prod_yx = jnp.einsum(form, left_y, right_x, precision=HIGHEST)  8.56 us
    dot_general x2, matrix products, spectral(): prod_xy = jnp.einsum(form, left_x, right_y, precision=HIGHEST)  7.53 us
  transfers between devices with their start and end apart: 4, of which 3 were waited for; matrix products, arithmetic and copies ran while one was open for 5% of the time, Pallas kernels for 0%

profile of v1, /device:TPU:12, one launch (start us, length us, event | category | flops | bytes accessed | tf_op | source)
XLA Modules:
  0.0 244.4 jit_solution(3560002869766204673)
XLA Ops:
  8.8 3.3 %multiply_select_fusion = (f32[384,384]{1,0:T(8,128)}, f32[384,384]{1,0:T(8,128)S(1)}) fusion(f32[384]{0:T(512)S(1)} %fusion.36, pred[384]{0:T(512)(128)(4,1)S(1)} %iota_compare_fusion.7), kind=kLoop, calls=%fused_computation.22 | loop fusion | flops 1916928 | bytes 1181568 | tf_op jit(solution)/shard_map/jit(_where)/select_n | solution.py:37
  12.2 2.7 %broadcast_multiply_fusion = (f32[8,64,768]{2,1,0:T(8,128)S(1)}, f32[8,64,768]{2,1,0:T(8,128)S(1)}) fusion(f32[768]{0:T(1024)S(1)} %fusion.31, f32[8,64,384]{2,1,0:T(8,128)S(1)} %copy-done.15, f32[384,384]{1,0:T(8,128)S(1)} %get-tuple-element.18, f32[384,384]{1,0:T(8,128)S(1)} %fusion.13), kind=kOutput, calls=%fused_computation.16 | convolution fusion | flops 1812627456 | bytes 5114880 | tf_op jit(solution)/shard_map/spt,tf->spf/dot_general | solution.py:73
  16.7 2.8 %copy.15 = f32[8,64,384]{1,0,2:T(8,128)} copy(f32[8,64,384]{2,1,0:T(8,128)} %get-tuple-element.21) | data formatting | bytes 1572864 | tf_op jit(solution)/shard_map/slice | solution.py:44
  19.4 3.8 %convolution_bitcast_fusion = f32[8,64,768]{2,1,0:T(8,128)S(1)} fusion(f32[8,64,384]{2,1,0:T(8,128)} %param.9, f32[384,384]{1,0:T(8,128)S(1)} %get-tuple-element.18, f32[384,384]{1,0:T(8,128)S(1)} %fusion.13), kind=kOutput, calls=%fused_computation.8 | convolution fusion | flops 1812234240 | bytes 3538944 | tf_op jit(solution)/shard_map/kpt,tf->kpf/dot_general | solution.py:74
  24.6 2.8 %copy.16 = f32[8,64,384]{1,0,2:T(8,128)} copy(f32[8,64,384]{2,1,0:T(8,128)} %get-tuple-element.12) | data formatting | bytes 1572864 | tf_op jit(solution)/shard_map/slice | solution.py:43
  27.4 2.8 %copy.23 = f32[8,64,384]{1,0,2:T(8,128)} copy(f32[8,64,384]{2,1,0:T(8,128)} %get-tuple-element.11) | data formatting | bytes 1572864 | tf_op jit(solution)/shard_map/slice | solution.py:43
  30.2 5.8 %fusion.51 = f32[384,8,8]{2,1,0:T(8,128)} fusion(f32[8,64,384]{1,0,2:T(8,128)} %copy.15, f32[8,64,384]{1,0,2:T(8,128)} %copy.16), kind=kOutput, calls=%fused_computation.86 | convolution fusion | flops 18874368 | bytes 1671168 | tf_op jit(solution)/shard_map/kpf,spf->ksf/dot_general | solution.py:46
  36.1 4.0 %fusion.52 = f32[384,8,8]{2,1,0:T(8,128)} fusion(f32[8,64,384]{1,0,2:T(8,128)S(1)} %copy-done.7, f32[8,64,384]{1,0,2:T(8,128)S(1)} %copy-done.8), kind=kOutput, calls=%fused_computation.87 | convolution fusion | flops 18874368 | bytes 1671168 | tf_op jit(solution)/shard_map/kpf,spf->ksf/dot_general | solution.py:47
  40.1 2.9 %copy.22 = f32[8,64,384]{1,0,2:T(8,128)} copy(f32[8,64,384]{2,1,0:T(8,128)} %get-tuple-element.22) | data formatting | bytes 1572864 | tf_op jit(solution)/shard_map/slice | solution.py:44
  43.0 6.4 %subtract_bitcast_fusion.1 = f32[8,8,384]{0,1,2:T(8,128)} fusion(f32[384,8,8]{2,1,0:T(8,128)} %fusion.51, f32[8,64,384]{1,0,2:T(8,128)} %copy.22, f32[8,64,384]{1,0,2:T(8,128)} %copy.23, f32[384]{0:T(512)S(1)} %fusion.38), kind=kOutput, calls=%fused_computation.7 | convolution fusion | flops 18923520 | bytes 1771008 | tf_op jit(solution)/shard_map/kpf,spf->ksf/dot_general | solution.py:45
  49.4 4.4 %add_bitcast_fusion.1 = f32[8,8,384]{0,1,2:T(8,128)} fusion(f32[384,8,8]{2,1,0:T(8,128)S(1)} %copy-done.4, f32[384,8,8]{2,1,0:T(8,128)S(1)} %copy-done.10, f32[8,64,384]{1,0,2:T(8,128)S(1)} %copy-done.5, f32[8,64,384]{1,0,2:T(8,128)S(1)} %copy-done.3, f32[384]{0:T(512)S(1)} %broadcast_subtract_fusion, f32[384]{0:T(512)S(1)} %fusion.38), kind=kOutput, calls=%fused_computation.6 | convolution fusion | flops 18972672 | bytes 1870848 | tf_op jit(solution)/shard_map/kpf,spf->ksf/dot_general | solution.py:48
  64.9 2.8 %copy.19 = f32[8,64,384]{1,0,2:T(8,128)} copy(f32[8,64,384]{2,1,0:T(8,128)} %get-tuple-element.8) | data formatting | bytes 1572864 | tf_op jit(solution)/shard_map/slice | solution.py:44
  67.7 2.8 %copy.27 = f32[8,64,384]{1,0,2:T(8,128)} copy(f32[8,64,384]{2,1,0:T(8,128)} %get-tuple-element.7) | data formatting | bytes 1572864 | tf_op jit(solution)/shard_map/slice | solution.py:44
  72.2 93.9 %all-gather.2.cloned.1.call-done = f32[32,64,384]{2,1,0:T(8,128)} async-done(((f32[1,64,384]{2,1,0:T(8,128)}), f32[32,64,384]{2,1,0:T(8,128)}) %all-gather.2.cloned.1.call-update) | async-done | bytes 3145744 | tf_op jit(solution)/shard_map/all_gather | solution.py:78
  166.1 2.7 %reduce_sum.20 = f32[64,384]{1,0:T(8,128)} reduce(f32[32,64,384]{2,1,0:T(8,128)} %all-gather.2.cloned.1.call-done, f32[]{:T(128)} %constant.85.clone.1), dimensions={0}, to_apply=%region_0.1 | reduce | flops 761856 | bytes 3244036 | tf_op jit(solution)/shard_map/reduce_sum | solution.py:78
  168.8 3.4 %fusion.24 = f32[64,4,384]{2,0,1:T(8,128)S(1)} fusion(f32[4,384,384]{2,1,0:T(8,128)S(1)} %copy-done, f32[64,384]{1,0:T(8,128)} %reduce_sum.20), kind=kOutput, calls=%fused_computation.43 | convolution fusion | flops 452984832 | bytes 2850816 | tf_op jit(solution)/shard_map/rt,but->rbu/dot_general | solution.py:64
  177.6 5.4 %fusion.53 = f32[384,64,8]{1,2,0:T(8,128)S(1)} fusion(f32[8,64,384]{1,0,2:T(8,128)} %copy.19, f32[8,8,384]{0,1,2:T(8,128)} %copy.29), kind=kOutput, calls=%fused_computation.88 | convolution fusion | flops 18874368 | bytes 1671168 | tf_op jit(solution)/shard_map/ksf,spf->kpf/dot_general | solution.py:46
  183.0 3.5 %fusion.54 = f32[384,64,8]{1,2,0:T(8,128)S(1)} fusion(f32[8,64,384]{1,0,2:T(8,128)S(1)} %copy-done.6, f32[8,8,384]{0,1,2:T(8,128)S(1)} %copy-done.9), kind=kOutput, calls=%fused_computation.89 | convolution fusion | flops 18874368 | bytes 1671168 | tf_op jit(solution)/shard_map/ksf,spf->kpf/dot_general | solution.py:47
  186.5 3.6 %subtract_bitcast_fusion = f32[8,64,384]{1,0,2:T(8,128)S(1)} fusion(f32[384,64,8]{1,2,0:T(8,128)S(1)} %fusion.53, f32[8,64,384]{1,0,2:T(8,128)S(1)} %copy-done.1, f32[8,8,384]{0,1,2:T(8,128)S(1)} %copy-done.9, f32[384]{0:T(512)S(1)} %fusion.38), kind=kOutput, calls=%fused_computation.5 | convolution fusion | flops 19267584 | bytes 2459136 | tf_op jit(solution)/shard_map/ksf,spf->kpf/dot_general | solution.py:45
  190.1 4.2 %add_bitcast_fusion = f32[8,64,384]{1,0,2:T(8,128)S(1)} fusion(f32[384,64,8]{1,2,0:T(8,128)S(1)} %fusion.53, f32[384,64,8]{1,2,0:T(8,128)S(1)} %fusion.54, f32[8,64,384]{1,0,2:T(8,128)S(1)} %copy-done.1, f32[8,8,384]{0,1,2:T(8,128)S(1)} %copy-done.2, f32[384]{0:T(512)S(1)} %broadcast_subtract_fusion, f32[384]{0:T(512)S(1)} %fusion.38), kind=kOutput, calls=%fused_computation.4 | convolution fusion | flops 19660800 | bytes 3247104 | tf_op jit(solution)/shard_map/ksf,spf->kpf/dot_general | solution.py:48
  195.6 6.6 %fusion = f32[8,64,384]{2,1,0:T(8,128)} fusion(f32[8,64,768]{1,0,2:T(8,128)S(1)} %pad_maximum_fusion, f32[384,384]{1,0:T(8,128)S(1)} %copy-done.13, f32[384,384]{1,0:T(8,128)S(1)} %copy-done.12), kind=kOutput, calls=%fused_computation.2 | convolution fusion | flops 1812529152 | bytes 3538944 | tf_op jit(solution)/shard_map/kpf,ft->kpt/dot_general | solution.py:89
  202.9 3.1 %collective-permute-start = (f32[1,16,384]{2,1,0:T(8,128)S(1)}, f32[1,16,384]{2,1,0:T(8,128)S(1)}, u32[]{:S(2)}, u32[]{:S(2)}) collective-permute-start(f32[1,16,384]{2,1,0:T(8,128)S(1)} %get-tuple-element.13), channel_id=1, source_target_pairs={{0,1},{1,2},{2,3},{3,4},{4,5},{5,6},{6,7},{7,8},{8,9},{9,10},{10,1... | collective-permute-start | bytes 73736 | tf_op jit(solution)/shard_map/ppermute | solution.py:16
  206.0 2.7 %collective-permute-start.1 = (f32[1,16,384]{2,1,0:T(8,128)S(1)}, f32[1,16,384]{2,1,0:T(8,128)S(1)}, u32[]{:S(2)}, u32[]{:S(2)}) collective-permute-start(f32[1,16,384]{2,1,0:T(8,128)S(1)} %get-tuple-element.14), channel_id=1, source_target_pairs={{1,0},{2,1},{3,2},{4,3},{5,4},{6,5},{7,6},{8,7},{9,8},{10,9},{11,1... | collective-permute-start | bytes 73736 | tf_op jit(solution)/shard_map/ppermute | solution.py:19
  212.9 22.7 %reduce-scatter.2.cloned.1.call-done = f32[1,64,384]{2,1,0:T(8,128)} async-done(((f32[8,64,384]{2,1,0:T(8,128)}), f32[1,64,384]{2,1,0:T(8,128)}) %reduce-scatter.2.cloned.1.call-update) | async-done | bytes 98320 | tf_op jit(solution)/shard_map/reduce_scatter | solution.py:88
  (80 shorter events, 31.3 us)
Async XLA Ops:
  6.5 162.3 %copy-start = (f32[4,384,384]{2,1,0:T(8,128)S(1)}, f32[4,384,384]{2,1,0:T(8,128)}, u32[]{:S(2)}) copy-start(f32[4,384,384]{2,1,0:T(8,128)} %param.12) | copy-start | bytes 7077892
  6.5 159.6 %all-gather.2.cloned.1.call-start = ((), (), s32[]{:S(2)}) async-start(), calls=%async_computation.1 | async-start | bytes 3244032 | tf_op jit(solution)/shard_map/all_gather | solution.py:78
  6.5 5.6 %copy-start.15 = (f32[8,64,384]{2,1,0:T(8,128)S(1)}, f32[8,64,384]{2,1,0:T(8,128)}, u32[]{:S(2)}) copy-start(f32[8,64,384]{2,1,0:T(8,128)} %param.8) | copy-start | bytes 2359300
  30.2 5.9 %copy-start.7 = (f32[8,64,384]{1,0,2:T(8,128)S(1)}, f32[8,64,384]{1,0,2:T(8,128)}, u32[]{:S(2)}) copy-start(f32[8,64,384]{1,0,2:T(8,128)} %copy.15) | copy-start | bytes 2359300
  30.2 5.9 %copy-start.8 = (f32[8,64,384]{1,0,2:T(8,128)S(1)}, f32[8,64,384]{1,0,2:T(8,128)}, u32[]{:S(2)}) copy-start(f32[8,64,384]{1,0,2:T(8,128)} %copy.23) | copy-start | bytes 2359300
  43.0 6.4 %copy-start.3 = (f32[8,64,384]{1,0,2:T(8,128)S(1)}, f32[8,64,384]{1,0,2:T(8,128)}, u32[]{:S(2)}) copy-start(f32[8,64,384]{1,0,2:T(8,128)} %copy.16) | copy-start | bytes 2359300
  43.0 6.4 %copy-start.4 = (f32[384,8,8]{2,1,0:T(8,128)S(1)}, f32[384,8,8]{2,1,0:T(8,128)}, u32[]{:S(2)}) copy-start(f32[384,8,8]{2,1,0:T(8,128)} %fusion.51) | copy-start | bytes 294916
  43.0 6.4 %copy-start.5 = (f32[8,64,384]{1,0,2:T(8,128)S(1)}, f32[8,64,384]{1,0,2:T(8,128)}, u32[]{:S(2)}) copy-start(f32[8,64,384]{1,0,2:T(8,128)} %copy.22) | copy-start | bytes 2359300
  43.0 6.4 %copy-start.10 = (f32[384,8,8]{2,1,0:T(8,128)S(1)}, f32[384,8,8]{2,1,0:T(8,128)}, u32[]{:S(2)}) copy-start(f32[384,8,8]{2,1,0:T(8,128)} %fusion.52) | copy-start | bytes 294916
  64.5 171.2 %reduce-scatter.2.cloned.1.call-start = ((), (), s32[]{:S(2)}) async-start(), calls=%async_computation.2 | async-start | bytes 884736 | tf_op jit(solution)/shard_map/reduce_scatter | solution.py:88
  67.7 2.8 %copy-start.20 = (f32[8]{0:T(128)S(1)}, f32[8]{0:T(128)}, u32[]{:S(2)}) copy-start(f32[8]{0:T(128)} %param.10) | copy-start | bytes 100
  168.8 3.4 %copy-start.16 = (f32[64,4]{1,0:T(8,128)S(1)}, f32[64,4]{1,0:T(8,128)}, u32[]{:S(2)}) copy-start(f32[64,4]{1,0:T(8,128)} %fusion.28) | copy-start | bytes 3076
  168.8 4.6 %copy-start.14 = (f32[64,384]{1,0:T(8,128)S(1)}, f32[64,384]{1,0:T(8,128)}, u32[]{:S(2)}) copy-start(f32[64,384]{1,0:T(8,128)} %reduce_sum.20) | copy-start | bytes 294916
  177.6 5.4 %copy-start.6 = (f32[8,64,384]{1,0,2:T(8,128)S(1)}, f32[8,64,384]{1,0,2:T(8,128)}, u32[]{:S(2)}) copy-start(f32[8,64,384]{1,0,2:T(8,128)} %copy.19) | copy-start | bytes 2359300
  177.6 5.4 %copy-start.9 = (f32[8,8,384]{0,1,2:T(8,128)S(1)}, f32[8,8,384]{0,1,2:T(8,128)}, u32[]{:S(2)}) copy-start(f32[8,8,384]{0,1,2:T(8,128)} %copy.28) | copy-start | bytes 294916
  183.0 3.5 %copy-start.1 = (f32[8,64,384]{1,0,2:T(8,128)S(1)}, f32[8,64,384]{1,0,2:T(8,128)}, u32[]{:S(2)}) copy-start(f32[8,64,384]{1,0,2:T(8,128)} %copy.27) | copy-start | bytes 2359300
  186.5 3.6 %copy-start.2 = (f32[8,8,384]{0,1,2:T(8,128)S(1)}, f32[8,8,384]{0,1,2:T(8,128)}, u32[]{:S(2)}) copy-start(f32[8,8,384]{0,1,2:T(8,128)} %copy.29) | copy-start | bytes 294916
  194.3 1.1 copy-start.12
  194.3 1.2 copy-start.13
  195.5 13.2 %copy-start.18 = (s32[4,64]{1,0:T(4,128)S(1)}, s32[4,64]{1,0:T(4,128)}, u32[]{:S(2)}) copy-start(s32[4,64]{1,0:T(4,128)} %param.15) | copy-start | bytes 3076
  202.9 7.8 %collective-permute-start = (f32[1,16,384]{2,1,0:T(8,128)S(1)}, f32[1,16,384]{2,1,0:T(8,128)S(1)}, u32[]{:S(2)}, u32[]{:S(2)}) collective-permute-start(f32[1,16,384]{2,1,0:T(8,128)S(1)} %get-tuple-element.13), channel_id=1, source_target_pairs={{0,1},{1,2},{2,3},{3,4},{4,5},{5,6},{6,7},{7,8},{8,9},{9,10},{10,1... | collective-permute-start | bytes 73736 | tf_op jit(solution)/shard_map/ppermute | solution.py:16
  206.0 5.7 %collective-permute-start.1 = (f32[1,16,384]{2,1,0:T(8,128)S(1)}, f32[1,16,384]{2,1,0:T(8,128)S(1)}, u32[]{:S(2)}, u32[]{:S(2)}) collective-permute-start(f32[1,16,384]{2,1,0:T(8,128)S(1)} %get-tuple-element.14), channel_id=1, source_target_pairs={{1,0},{2,1},{3,2},{4,3},{5,4},{6,5},{7,6},{8,7},{9,8},{10,9},{11,1... | collective-permute-start | bytes 73736 | tf_op jit(solution)/shard_map/ppermute | solution.py:19
  211.8 1.0 copy-start.17
  211.8 23.9 %copy-start.19 = (f32[64]{0:T(128)S(1)}, f32[64]{0:T(128)}, u32[]{:S(2)}) copy-start(f32[64]{0:T(128)} %param.13) | copy-start | bytes 772
  (1 other events, 0.8 us)
Sparse Core Ops, SparseCore 0:
  64.6 101.4 all-gather.1
  202.3 33.3 reduce-scatter.1
